TPU v7x, 32 devices: a whole 2x2x4 slice. The times are simulated.
32 devices in a mesh: seq: 16 (over z, y, x), head: 2 (over core).
Axes of the slice: x: 2, y: 2, z: 4, core: 2. Of those that a mesh axis runs over, the one named last changes fastest.
Arguments:
- tokens: bfloat16 [4096, 768], P('seq', 'head'), may hold values from -6 to 6
- w_query: bfloat16 [768, 512], P(None, 'head'), may hold values from -0.21875 to 0.21875
- w_key: bfloat16 [768, 512], P(None, 'head'), may hold values from -0.21875 to 0.21875
- w_value: bfloat16 [768, 512], P(None, 'head'), may hold values from -0.21875 to 0.21875
- w_out: bfloat16 [512, 768], P('head'), may hold values from -0.25 to 0.25
- feature_dirs: float32 [64, 128], replicated, may hold values from -5 to 5
- kernel_taps: bfloat16 [8, 129], P('head'), may hold values from -0.3984375 to 0.3984375
Outputs:
- mixed: bfloat16 [4096, 768], P('seq', 'head')
- key_mixed: bfloat16 [4096, 512], P('seq', 'head')
All inputs are finite; a program needn't handle non-finite values.
Results may differ from a plain program's by a relative error of at most 0.018.
Values may be sent and summed in bfloat16 or wider, within the bound.
A program may use at most 64 MiB of HBM per device.

v0:
```python
import jax
import jax.numpy as jnp
from jax import lax
from jax.sharding import PartitionSpec as P

HEAD_DIM = 64


def padded(cells, sides, width):
    for axis, dim in sides:
        count = lax.axis_size(axis)
        ends = count - 1
        head = lax.slice_in_dim(cells, 0, width, axis=dim)
        tail = lax.slice_in_dim(cells, cells.shape[dim] - width, cells.shape[dim], axis=dim)
        cells = jnp.concatenate(
            [
                lax.ppermute(tail, axis, [(i, (i + 1) % count) for i in range(ends)]),
                cells,
                lax.ppermute(head, axis, [((i + 1) % count, i) for i in range(ends)]),
            ],
            axis=dim,
        )
    return cells


def build_band(taps, block):
    reach = (taps.shape[1] - 1) // 2
    width = block + 2 * reach
    padded_taps = jnp.pad(taps, ((0, 0), (0, width + 1 - taps.shape[1])))
    tiled = jnp.tile(padded_taps, (1, block))
    return tiled[:, : block * width].reshape(taps.shape[0], block, width)


def band_conv(keys_ext, band, blocks, block):

    def one_block(index):
        return jnp.einsum("hij,jhd->ihd", band, keys_ext, preferred_element_type=jnp.float32)

    result = lax.map(one_block, jnp.arange(blocks, dtype=jnp.int32))
    return result.reshape(blocks * block, keys_ext.shape[1], keys_ext.shape[2])


def body(tokens, w_query, w_key, w_value, w_out, feature_dirs, kernel_taps):
    highest = lax.Precision.HIGHEST
    reach = (kernel_taps.shape[1] - 1) // 2
    token_count = tokens.shape[0]
    heads_here = w_query.shape[1] // HEAD_DIM
    block = min(512, token_count)
    key_scale = HEAD_DIM ** (-0.25)
    gathered = lax.all_gather(tokens, "head", axis=1, tiled=True)
    queries = jnp.dot(gathered, w_query, preferred_element_type=jnp.float32).astype(jnp.bfloat16)
    values = jnp.dot(gathered, w_value, preferred_element_type=jnp.float32).astype(jnp.bfloat16)
    keys = jnp.dot(gathered, w_key, preferred_element_type=jnp.float32).astype(jnp.bfloat16)
    keys_ext = padded(keys, (("seq", 0),), reach)
    keys_ext = keys_ext.reshape(token_count + 2 * reach, heads_here, HEAD_DIM)
    band = build_band(kernel_taps, block)
    conv_keys = band_conv(keys_ext, band, token_count // block, block)
    key_mixed = conv_keys.reshape(token_count, heads_here * HEAD_DIM).astype(jnp.bfloat16)
    scaled_keys = conv_keys * key_scale
    key_logits = jnp.einsum("thd,df->thf", scaled_keys, feature_dirs, precision=highest)
    key_feats = jnp.exp(
        key_logits - 0.5 * jnp.sum(scaled_keys * scaled_keys, axis=2, keepdims=True)
    ).astype(jnp.bfloat16)
    scaled_queries = (
        queries.reshape(token_count, heads_here, HEAD_DIM).astype(jnp.float32) * key_scale
    )
    query_feats = jnp.exp(
        jnp.einsum("thd,df->thf", scaled_queries, feature_dirs, precision=highest)
    ).astype(jnp.bfloat16)
    values_three = values.reshape(token_count, heads_here, HEAD_DIM)
    state = jnp.einsum("thf,thd->fhd", key_feats, values_three, preferred_element_type=jnp.float32)
    state = state.reshape(key_feats.shape[2], heads_here * HEAD_DIM)
    normal = jnp.sum(key_feats.astype(jnp.float32), axis=0)
    state, normal = lax.psum((state, normal), "seq")
    state_b = state.astype(jnp.bfloat16).reshape(key_feats.shape[2], heads_here, HEAD_DIM)
    normal_b = normal.astype(jnp.bfloat16)
    numer = jnp.einsum("thf,fhd->thd", query_feats, state_b, preferred_element_type=jnp.float32)
    denom = jnp.einsum("thf,hf->th", query_feats, normal_b, preferred_element_type=jnp.float32)
    attended = (
        (numer / denom[:, :, None]).reshape(token_count, heads_here * HEAD_DIM).astype(jnp.bfloat16)
    )
    full_rows = lax.all_to_all(w_out, "head", split_axis=1, concat_axis=0, tiled=True)
    summed = jnp.dot(
        lax.all_gather(attended, "head", axis=1, tiled=True),
        full_rows,
        preferred_element_type=jnp.float32,
    )
    return (summed.astype(jnp.bfloat16), key_mixed)


def solution(mesh):
    return jax.shard_map(
        body,
        mesh=mesh,
        in_specs=(
            P("seq", "head"),
            P(None, "head"),
            P(None, "head"),
            P(None, "head"),
            P("head", None),
            P(),
            P("head", None),
        ),
        out_specs=(P("seq", "head"), P("seq", "head")),
        check_vma=False,
    )
```

profile of v0, /device:TPU:0, one launch (start us, length us, event | category | flops | bytes accessed | tf_op | source)
XLA Modules:
  0.0 106.6 jit_solution(10738542902392752106)
XLA Ops:
  0.6 0.0 copy-start
  0.6 2.6 %all_gather.6 = bf16[256,768]{1,0:T(8,128)(2,1)S(1)} all-gather(bf16[256,384]{1,0:T(8,128)(2,1)} %param.7), channel_id=1, replica_groups=mesh['seq'=16,'head'=2] {'head'}, dimensions={1}, use_global_device_ids=true | all-gather | bytes 589824 | tf_op jit(solution)/shard_map/all_gather | solution.py:50
  3.2 0.0 copy-done
  3.2 0.3 convolution_convert_fusion.2
  3.5 4.8 %collective-permute-start = (bf16[64,256]{1,0:T(8,128)(2,1)S(1)}, bf16[64,256]{1,0:T(8,128)(2,1)S(1)}, u32[]{:S(2)}, u32[]{:S(2)}) collective-permute-start(bf16[64,256]{1,0:T(8,128)(2,1)S(1)} %get-tuple-element.22), channel_id=1, source_target_pairs={{0,2},{2,4},{4,6},{6,8},{8,10},{10,12},{12,14},{14,16},{16,18},{18... | collective-permute-start | bytes 98312 | tf_op jit(solution)/shard_map/ppermute | solution.py:17
  8.2 1.3 %collective-permute-start.1 = (bf16[64,256]{1,0:T(8,128)(2,1)S(1)}, bf16[64,256]{1,0:T(8,128)(2,1)S(1)}, u32[]{:S(2)}, u32[]{:S(2)}) collective-permute-start(bf16[64,256]{1,0:T(8,128)(2,1)S(1)} %get-tuple-element.23), channel_id=1, source_target_pairs={{2,0},{4,2},{6,4},{8,6},{10,8},{12,10},{14,12},{16,14},{18,16},{20... | collective-permute-start | bytes 98312 | tf_op jit(solution)/shard_map/ppermute | solution.py:19
  9.6 0.9 copy.14
  10.5 3.6 %all-to-all-start = ((bf16[256,2,384]{0,2,1:T(8,128)(2,1)}), bf16[256,2,384]{0,2,1:T(8,128)(2,1)S(1)}, u32[]{:S(2)}, u32[]{:S(2)}) async-start(bf16[256,2,384]{0,2,1:T(8,128)(2,1)} %bitcast.13), calls=%async_computation | async-start | bytes 786432 | tf_op jit(solution)/shard_map/all_to_all | solution.py:82
  14.1 0.0 copy-start.4
  14.1 0.3 convolution_convert_fusion.3
  14.5 0.7 copy-done.4
  15.1 0.3 fusion.6
  15.4 0.4 copy-done.5
  15.9 1.0 fusion.2
  16.9 0.1 tile.4
  17.0 1.6 %tile.10 = bf16[4,98560]{1,0:T(4,128)(2,1)S(1)} reshape(bf16[4,256,385]{2,1,0:T(8,128)(2,1)S(1)} %tile.4) | data formatting | bytes 1576960 | tf_op jit(solution)/shard_map/tile | solution.py:30
  18.6 0.9 copy-done.1
  19.4 0.0 all-to-all-done
  19.5 0.2 copy.15
  19.7 0.0 collective-permute-done
  19.7 0.0 collective-permute-done.1
  19.7 0.2 copy.13
  19.9 0.7 slice-done
  20.6 0.4 fusion.11
  21.0 1.1 convert_reduce_fusion
  22.1 0.2 fusion.20
  22.3 80.2 %all-reduce.3 = (bf16[128,256]{0,1:T(8,128)(2,1)S(1)}, bf16[4,128]{1,0:T(4,128)(2,1)S(1)}) all-reduce(f32[128,256]{0,1:T(8,128)S(1)} %bitcast.70, f32[4,128]{1,0:T(4,128)S(1)} %get-tuple-element.26), channel_id=1, replica_groups=mesh['seq'=16,'head'=2] {'seq'}, use_global_device_ids=true, to_apply=%region_1.2 | all-reduce | flops 33280 | bytes 199680 | tf_op jit(solution)/shard_map/psum | solution.py:74
  102.5 0.2 fusion.16
  102.6 0.2 fusion.4
  102.9 2.0 %all_gather.7 = bf16[256,512]{0,1:T(8,128)(2,1)S(1)} all-gather(bf16[256,256]{0,1:T(8,128)(2,1)S(1)} %bitcast.72), channel_id=1, replica_groups=mesh['seq'=16,'head'=2] {'head'}, dimensions={1}, use_global_device_ids=true | all-gather | bytes 393216 | tf_op jit(solution)/shard_map/all_gather | solution.py:84
  104.9 0.8 copy.16
  105.6 1.0 convolution_convert_fusion
  (15 shorter events, 0.1 us)
Async XLA Ops:
  0.6 2.6 %copy-start = (bf16[768,256]{1,0:T(8,128)(2,1)S(1)}, bf16[768,256]{1,0:T(8,128)(2,1)}, u32[]{:S(2)}) copy-start(bf16[768,256]{1,0:T(8,128)(2,1)} %param.9) | copy-start | bytes 1179652
  3.2 6.4 %copy-start.3 = (bf16[256,768]{1,0:T(8,128)(2,1)S(1)}, bf16[256,768]{1,0:T(8,128)(2,1)}, u32[]{:S(2)}) copy-start(bf16[256,768]{1,0:T(8,128)(2,1)} %param.11) | copy-start | bytes 1179652
  3.5 16.2 %collective-permute-start = (bf16[64,256]{1,0:T(8,128)(2,1)S(1)}, bf16[64,256]{1,0:T(8,128)(2,1)S(1)}, u32[]{:S(2)}, u32[]{:S(2)}) collective-permute-start(bf16[64,256]{1,0:T(8,128)(2,1)S(1)} %get-tuple-element.22), channel_id=1, source_target_pairs={{0,2},{2,4},{4,6},{6,8},{8,10},{10,12},{12,14},{14,16},{16,18},{18... | collective-permute-start | bytes 98312 | tf_op jit(solution)/shard_map/ppermute | solution.py:17
  8.2 11.4 %collective-permute-start.1 = (bf16[64,256]{1,0:T(8,128)(2,1)S(1)}, bf16[64,256]{1,0:T(8,128)(2,1)S(1)}, u32[]{:S(2)}, u32[]{:S(2)}) collective-permute-start(bf16[64,256]{1,0:T(8,128)(2,1)S(1)} %get-tuple-element.23), channel_id=1, source_target_pairs={{2,0},{4,2},{6,4},{8,6},{10,8},{12,10},{14,12},{16,14},{18,16},{20... | collective-permute-start | bytes 98312 | tf_op jit(solution)/shard_map/ppermute | solution.py:19
  10.5 3.6 %copy-start.2 = (bf16[768,256]{1,0:T(8,128)(2,1)S(1)}, bf16[768,256]{1,0:T(8,128)(2,1)}, u32[]{:S(2)}) copy-start(bf16[768,256]{1,0:T(8,128)(2,1)} %param.10) | copy-start | bytes 1179652
  10.5 9.0 %all-to-all-start = ((bf16[256,2,384]{0,2,1:T(8,128)(2,1)}), bf16[256,2,384]{0,2,1:T(8,128)(2,1)S(1)}, u32[]{:S(2)}, u32[]{:S(2)}) async-start(bf16[256,2,384]{0,2,1:T(8,128)(2,1)} %bitcast.13), calls=%async_computation | async-start | bytes 786432 | tf_op jit(solution)/shard_map/all_to_all | solution.py:82
  14.1 1.0 copy-start.4
  15.1 0.8 copy-start.5
  15.9 1.0 copy-start.6
  18.6 0.9 copy-start.1
  19.5 1.1 %slice-start = ((bf16[4,98560]{1,0:T(4,128)(2,1)}), bf16[4,98304]{1,0:T(4,128)(2,1)S(1)}, s32[]{:S(2)}) async-start(bf16[4,98560]{1,0:T(4,128)(2,1)} %copy-done.1), calls=%async_computation.1 | async-start | bytes 1572864 | tf_op jit(solution)/shard_map/slice | solution.py:31
where the time goes:
time: 107 us
  blocking collectives  84.7 us (79%)
  starting transfers between devices  9.64 us (9%)
  local copies, waits for them, and re-layouts  6.43 us (6%)
  matrix products  4.93 us (5%)
    psum x1, blocking collectives, body(): state, normal = lax.psum((state, normal), 'seq')  80.2 us
    ppermute x1, starting transfers between devices, padded(): lax.ppermute(tail, axis, [(i, (i + 1) % count) for i in range(ends)])  4.75 us
    unnamed x16, local copies, waits for them, and re-layouts  3.7 us
    all_to_all x1, starting transfers between devices, body(): lax.all_to_all(w_out, 'head', split_axis=1, concat_axis=0, tiled=True)  3.6 us
    all_gather x1, blocking collectives, body(): gathered = lax.all_gather(tokens, 'head', axis=1, tiled=True)  2.55 us
  transfers between devices with their start and end apart: 3, of which 0 were waited for; matrix products, arithmetic and copies ran while one was open for 4% of the time, Pallas kernels for 0%

commit v1 on v0

v1 whole, which is shorter than its diff:
```python
import functools

import jax
import jax.numpy as jnp
from jax import lax
from jax.experimental import pallas as pl
from jax.experimental.pallas import tpu as pltpu
from jax.sharding import PartitionSpec as P

HEAD_DIM = 64
LANES = 128
PAD = 16
MESH = pl.DeviceIdType.MESH
F32, BF16 = jnp.float32, jnp.bfloat16


def mm(a, b):
    return jnp.dot(a, b, preferred_element_type=F32)


def mm_nt(a, b):
    return lax.dot_general(a, b, (((1,), (1,)), ((), ())), preferred_element_type=F32)


def split(value):
    high = value.astype(BF16)
    return high, (value - high.astype(F32)).astype(BF16)


def fused(
    n, heads, reach, tok, wq, wk, wv, wo, dirs, taps, mixed, key_mixed,
    x, q_w, k_w, v_w, o_w, dirs_v, taps_v, taps_pad, band, dirs_hi, dirs_lo, norm_w,
    keys, conv, kmix, vt, queries, qf, part, part_b, inner_in, outer_b, outer_in, full, gate, att, out_v,
    loc, send, recv, inner_send, inner_recv, outer_send, outer_recv, full_send, full_recv,
):
    rows, half = tok.shape
    features = dirs.shape[1]
    out_cols = mixed.shape[1]
    width = heads * HEAD_DIM
    pairs = width // LANES
    group, block = heads, 2 * reach
    outer = n // group
    scale = HEAD_DIM ** (-0.25)
    me, core = lax.axis_index("seq"), lax.axis_index("head")
    other = 1 - core
    spot, plane = lax.rem(me, group), lax.div(me, group)

    def inner_peer(d):
        return plane * group + lax.rem(spot + d, group)

    def outer_peer(e):
        return lax.rem(plane + e, outer) * group + spot

    barrier = pltpu.get_barrier_semaphore()

    def greet(seq_id, core_id):
        pl.semaphore_signal(barrier, inc=1, device_id=(seq_id, core_id), device_id_type=MESH)

    for e in range(1, outer):
        greet(outer_peer(e), core)

    @pl.when(me > 0)
    def _():
        greet(me - 1, core)
        greet(me - 1, other)

    @pl.when(me < n - 1)
    def _():
        greet(me + 1, core)
        greet(me + 1, other)

    for d in range(1, group):
        greet(inner_peer(d), core)
    greet(me, other)

    own_cols = pl.ds(pl.multiple_of(core * half, LANES), half)
    main = pl.ds(reach, rows)
    my_out = pl.ds(pl.multiple_of(core * out_cols, LANES), out_cols)
    other_out = pl.ds(pl.multiple_of(other * out_cols, LANES), out_cols)
    local = [
        pltpu.make_async_copy(src, dst, loc.at[at])
        for at, (src, dst) in enumerate(
            [
                (tok, x.at[main, own_cols]),
                (wk, k_w),
                (wv, v_w),
                (dirs, dirs_v),
                (taps, taps_v),
                (wq, q_w),
                (wo.at[:, my_out], o_w.at[core]),
            ]
        )
    ]
    for copy in local:
        copy.start()

    @pl.when(me == 0)
    def _():
        x[0:reach, :] = jnp.zeros((reach, x.shape[1]), BF16)

    @pl.when(me == n - 1)
    def _():
        x[reach + rows :, :] = jnp.zeros((reach, x.shape[1]), BF16)

    sides = 2 * ((me > 0).astype(jnp.int32) + (me < n - 1).astype(jnp.int32))
    pl.semaphore_wait(barrier, outer - 1 + group + sides)

    def remote(src, dst, at, seq_id, core_id):
        return pltpu.make_async_remote_copy(
            src_ref=src, dst_ref=dst, send_sem=send.at[at], recv_sem=recv.at[at],
            device_id=(seq_id, core_id), device_id_type=MESH,
        )

    swap_tok = remote(tok, x.at[main, own_cols], 0, me, other)
    lower = [
        remote(tok.at[pl.ds(0, reach), :], x.at[pl.ds(reach + rows, reach), own_cols], 1 + k, me - 1, c)
        for k, c in enumerate((core, other))
    ]
    upper = [
        remote(tok.at[pl.ds(rows - reach, reach), :], x.at[pl.ds(0, reach), own_cols], 3 + k, me + 1, c)
        for k, c in enumerate((core, other))
    ]
    swap_out = remote(wo.at[:, other_out], o_w.at[core], 5, me, other)

    @pl.when(me > 0)
    def _():
        for copy in lower:
            copy.start()

    @pl.when(me < n - 1)
    def _():
        for copy in upper:
            copy.start()

    swap_tok.start()
    swap_out.start()

    dirs_hi[...] = jnp.zeros(dirs_hi.shape, BF16)
    dirs_lo[...] = jnp.zeros(dirs_lo.shape, BF16)
    norm_w[...] = jnp.zeros(norm_w.shape, BF16)
    gate[...] = jnp.zeros(gate.shape, BF16)
    taps_pad[...] = jnp.zeros(taps_pad.shape, F32)
    for h in range(heads):
        r, c = slice(h * HEAD_DIM, (h + 1) * HEAD_DIM), slice(h * features, (h + 1) * features)
        norm_w[r, c] = jnp.full((HEAD_DIM, features), 0.5 * HEAD_DIM ** (-0.5), BF16)
        vt[h, HEAD_DIM:, :] = jnp.ones((PAD, rows), BF16)
    local[3].wait()
    dir_high, dir_low = split(dirs_v[...] * scale)
    for h in range(heads):
        r, c = slice(h * HEAD_DIM, (h + 1) * HEAD_DIM), slice(h * features, (h + 1) * features)
        dirs_hi[r, c] = dir_high
        dirs_lo[r, c] = dir_low
    local[4].wait()
    taps_pad[0:heads, 0 : block + 1] = taps_v[...].astype(F32)
    for h in range(heads):
        row = jnp.broadcast_to(taps_pad[h : h + 1, :], (block, 2 * block))
        band[h * block : (h + 1) * block, :] = pltpu.roll(row, 0, 1, stride=1, stride_axis=0).astype(BF16)

    local[0].wait()
    local[1].wait()
    swap_tok.wait_recv()
    keys[reach : reach + rows, :] = mm(x[reach : reach + rows, :], k_w[...]).astype(BF16)
    local[2].wait()
    values_t = mm(x[reach : reach + rows, :], v_w[...]).T.astype(BF16)
    for h in range(heads):
        vt[h, 0:HEAD_DIM, :] = values_t[h * HEAD_DIM : (h + 1) * HEAD_DIM, :]

    @pl.when(me > 0)
    def _():
        for copy in upper:
            copy.wait_recv()

    @pl.when(me < n - 1)
    def _():
        for copy in lower:
            copy.wait_recv()

    keys[0:reach, :] = mm(x[0:reach, :], k_w[...]).astype(BF16)
    keys[reach + rows :, :] = mm(x[reach + rows :, :], k_w[...]).astype(BF16)

    lane = lax.broadcasted_iota(jnp.int32, (block, LANES), 1)
    for b in range(rows // block):
        for p in range(pairs):
            got = mm(
                band[2 * p * block : 2 * (p + 1) * block, :],
                keys[b * block : (b + 2) * block, p * LANES : (p + 1) * LANES],
            )
            conv[b * block : (b + 1) * block, p * LANES : (p + 1) * LANES] = jnp.where(
                lane < HEAD_DIM, got[:block], got[block:]
            )
    c = conv[...]
    c_hi, c_lo = split(c)
    kmix[...] = c_hi
    sq_hi, sq_lo = split(c * c)
    out_keys = pltpu.make_async_copy(kmix, key_mixed, loc.at[7])
    out_keys.start()
    logits = mm(c_hi, dirs_hi[...]) + mm(c_lo, dirs_hi[...]) + mm(c_hi, dirs_lo[...])
    logits = logits - (mm(sq_hi, norm_w[...]) + mm(sq_lo, norm_w[...]))
    kf = jnp.exp(logits).astype(BF16)
    for h in range(heads):
        got = mm(vt[h], kf[:, h * features : (h + 1) * features])
        part[h] = got
        part_b[h] = got.astype(BF16)

    scatter = [
        pltpu.make_async_remote_copy(
            src_ref=part_b.at[lax.rem(spot + d, group)], dst_ref=inner_in.at[d - 1],
            send_sem=inner_send.at[d - 1], recv_sem=inner_recv.at[d - 1],
            device_id=(inner_peer(d), core), device_id_type=MESH,
        )
        for d in range(1, group)
    ]
    for copy in scatter:
        copy.start()
    local[5].wait()
    queries[...] = mm(x[reach : reach + rows, :], q_w[...]).astype(BF16)
    mine = part[spot]
    for d in range(1, group):
        scatter[d - 1].wait_recv()
        mine = mine + inner_in[d - 1].astype(F32)
    outer_b[...] = mine.astype(BF16)
    spread = [
        pltpu.make_async_remote_copy(
            src_ref=outer_b, dst_ref=outer_in.at[e - 1],
            send_sem=outer_send.at[e - 1], recv_sem=outer_recv.at[e - 1],
            device_id=(outer_peer(e), core), device_id_type=MESH,
        )
        for e in range(1, outer)
    ]
    for copy in spread:
        copy.start()
    q = queries[...]
    qf[...] = jnp.exp(mm(q, dirs_hi[...]) + mm(q, dirs_lo[...])).astype(BF16)
    for e in range(1, outer):
        spread[e - 1].wait_recv()
        mine = mine + outer_in[e - 1].astype(F32)
    full[spot] = mine.astype(BF16)
    gather = [
        pltpu.make_async_remote_copy(
            src_ref=full.at[spot], dst_ref=full.at[spot],
            send_sem=full_send.at[d - 1], recv_sem=full_recv.at[d - 1],
            device_id=(inner_peer(d), core), device_id_type=MESH,
        )
        for d in range(1, group)
    ]
    for copy in gather:
        copy.start()
    for copy in gather:
        copy.wait_recv()

    for h in range(heads):
        p, k = divmod(h, 2)
        r = slice(k * HEAD_DIM, (k + 1) * HEAD_DIM)
        s = slice(LANES + k * HEAD_DIM, LANES + (k + 1) * HEAD_DIM)
        f = slice(k * features, (k + 1) * features)
        gate[p, r, f] = full[h, 0:HEAD_DIM, :]
        gate[p, s, f] = jnp.concatenate([full[h, HEAD_DIM:, :]] * (HEAD_DIM // PAD), axis=0)
    steps = 2
    span = rows // steps
    swap_att = []
    for b in range(steps):
        r = slice(b * span, (b + 1) * span)
        for p in range(pairs):
            got = mm_nt(qf[r, 2 * p * features : 2 * (p + 1) * features], gate[p])
            att[core, r, p * LANES : (p + 1) * LANES] = (got[:, :LANES] / got[:, LANES:]).astype(BF16)
        piece = att.at[core, pl.ds(b * span, span), :]
        copy = remote(piece, piece, 6 + b, me, other)
        copy.start()
        swap_att.append(copy)
    local[6].wait()
    own = [mm(att[core, b * span : (b + 1) * span, :], o_w[core]) for b in range(steps)]
    swap_out.wait_recv()
    outs = []
    for b in range(steps):
        r = slice(b * span, (b + 1) * span)
        swap_att[b].wait_recv()
        out_v[r, :] = (own[b] + mm(att[other, r, :], o_w[other])).astype(BF16)
        copy = pltpu.make_async_copy(
            out_v.at[pl.ds(b * span, span), :], mixed.at[pl.ds(b * span, span), :], loc.at[8 + b]
        )
        copy.start()
        outs.append(copy)

    for copy in [swap_tok, swap_out] + scatter + spread + gather + swap_att:
        copy.wait_send()

    @pl.when(me > 0)
    def _():
        for copy in lower:
            copy.wait_send()

    @pl.when(me < n - 1)
    def _():
        for copy in upper:
            copy.wait_send()

    out_keys.wait()
    for copy in outs:
        copy.wait()


def body(n, tokens, w_query, w_key, w_value, w_out, feature_dirs, kernel_taps):
    rows, half = tokens.shape
    d = w_key.shape[0]
    width = w_key.shape[1]
    heads = width // HEAD_DIM
    features = feature_dirs.shape[1]
    reach = (kernel_taps.shape[1] - 1) // 2
    block = 2 * reach
    out_cols = w_out.shape[1] // 2
    outer = n // heads
    chunk = HEAD_DIM + PAD
    vmem = pltpu.VMEM
    dma = pltpu.SemaphoreType.DMA
    any_spec = pl.BlockSpec(memory_space=pl.ANY)
    return pl.pallas_call(
        functools.partial(fused, n, heads, reach),
        out_shape=(
            jax.ShapeDtypeStruct((rows, out_cols), BF16),
            jax.ShapeDtypeStruct((rows, width), BF16),
        ),
        in_specs=[any_spec] * 7,
        out_specs=(any_spec, any_spec),
        scratch_shapes=[
            vmem((rows + 2 * reach, d), BF16),
            vmem((d, width), BF16),
            vmem((d, width), BF16),
            vmem((d, width), BF16),
            vmem((2, width, out_cols), BF16),
            vmem(feature_dirs.shape, F32),
            vmem(kernel_taps.shape, BF16),
            vmem((8, 2 * block), F32),
            vmem((heads * block, 2 * block), BF16),
            vmem((width, heads * features), BF16),
            vmem((width, heads * features), BF16),
            vmem((width, heads * features), BF16),
            vmem((rows + 2 * reach, width), BF16),
            vmem((rows, width), F32),
            vmem((rows, width), BF16),
            vmem((heads, chunk, rows), BF16),
            vmem((rows, width), BF16),
            vmem((rows, heads * features), BF16),
            vmem((heads, chunk, features), F32),
            vmem((heads, chunk, features), BF16),
            vmem((heads - 1, chunk, features), BF16),
            vmem((chunk, features), BF16),
            vmem((max(outer - 1, 1), chunk, features), BF16),
            vmem((heads, chunk, features), BF16),
            vmem((width // LANES, 2 * LANES, 2 * features), BF16),
            vmem((2, rows, width), BF16),
            vmem((rows, out_cols), BF16),
            dma((10,)),
            dma((8,)),
            dma((8,)),
            dma((heads - 1,)),
            dma((heads - 1,)),
            dma((max(outer - 1, 1),)),
            dma((max(outer - 1, 1),)),
            dma((heads - 1,)),
            dma((heads - 1,)),
        ],
        compiler_params=pltpu.CompilerParams(collective_id=0, has_side_effects=True),
        name="fused",
    )(tokens, w_query, w_key, w_value, w_out, feature_dirs, kernel_taps)


def solution(mesh):
    return jax.shard_map(
        functools.partial(body, mesh.shape["seq"]),
        mesh=mesh,
        in_specs=(
            P("seq", "head"),
            P(None, "head"),
            P(None, "head"),
            P(None, "head"),
            P("head", None),
            P(),
            P("head", None),
        ),
        out_specs=(P("seq", "head"), P("seq", "head")),
        check_vma=False,
    )
```

time: 107 us -> 28.6 us (0.27)
  the two profiles are of different devices: /device:TPU:0 before, /device:TPU:1 now
where the time goes in v1:
time: 28.6 us; the launch traced here: 28.4 us
  Pallas kernels  25.5 us (89%)
  local copies, waits for them, and re-layouts  2.32 us (8%)
  between operations  0.65 us (2%)
    pallas_call x1, Pallas kernels, body(): pl.pallas_call(functools.partial(fused, n, heads, reach), out_shape=(jax....  25.5 us
    unnamed x4, local copies, waits for them, and re-layouts  2.32 us

profile of v1, /device:TPU:1, one launch (start us, length us, event | category | flops | bytes accessed | tf_op | source)
XLA Modules:
  0.0 28.4 jit_solution(14113395353580442077)
XLA Ops:
  0.6 25.5 %fused.1 = (bf16[256,384]{1,0:T(8,128)(2,1)}, bf16[256,256]{1,0:T(8,128)(2,1)}) custom-call(bf16[256,384]{1,0:T(8,128)(2,1)} %tok.1, bf16[768,256]{1,0:T(8,128)(2,1)} %wq.1, bf16[768,256]{1,0:T(8,128)(2,1)} %wk.1, bf16[768,256]{1,0:T(8,128)(2,1)} %wv.1, bf16[256,768]{1,0:T(8,128)(2,1)} %wo.1, f32[64,128]{1,0:T(8,128)} %dirs.1, bf16[4,129]{1,0:T(4,128)(2,1)} %taps.1), custom_call_target="tpu_custom_call" | custom-call | tf_op jit(solution)/shard_map/fused/pallas_call | solution.py:316
  26.1 0.0 copy-start
  26.1 1.7 %copy.11 = bf16[256,384]{1,0:T(8,128)(2,1)} copy(bf16[256,384]{1,0:T(8,128)(2,1)} %get-tuple-element.4) | data formatting | bytes 393216
  27.8 0.0 copy-done
  27.8 0.7 %copy.12 = bf16[256,256]{1,0:T(8,128)(2,1)} copy(bf16[256,256]{1,0:T(8,128)(2,1)S(1)} %copy-done) | data formatting | bytes 262144
Async XLA Ops:
  26.1 1.7 %copy-start = (bf16[256,256]{1,0:T(8,128)(2,1)S(1)}, bf16[256,256]{1,0:T(8,128)(2,1)}, u32[]{:S(2)}) copy-start(bf16[256,256]{1,0:T(8,128)(2,1)} %get-tuple-element.5) | copy-start | bytes 393220

commit v2 on v1

--- a/solution.py
+++ b/solution.py
@@ -9,7 +9,7 @@
 
 HEAD_DIM = 64
 LANES = 128
-PAD = 16
+PAD = 8
 MESH = pl.DeviceIdType.MESH
 F32, BF16 = jnp.float32, jnp.bfloat16
 
@@ -28,14 +28,14 @@
 
 
 def fused(
-    n, heads, reach, tok, wq, wk, wv, wo, dirs, taps, mixed, key_mixed,
+    n, heads, reach, tok, wq, wk, wv, wo, dirs, taps, part_out, att_in, o_w_in, kmix,
     x, q_w, k_w, v_w, o_w, dirs_v, taps_v, taps_pad, band, dirs_hi, dirs_lo, norm_w,
-    keys, conv, kmix, vt, queries, qf, part, part_b, inner_in, outer_b, outer_in, full, gate, att, out_v,
+    keys, conv, vt, queries, qf, part, part_b, inner_in, outer_b, outer_in, full, gate, att,
     loc, send, recv, inner_send, inner_recv, outer_send, outer_recv, full_send, full_recv,
 ):
     rows, half = tok.shape
     features = dirs.shape[1]
-    out_cols = mixed.shape[1]
+    out_cols = part_out.shape[1]
     width = heads * HEAD_DIM
     pairs = width // LANES
     group, block = heads, 2 * reach
@@ -62,12 +62,10 @@
     @pl.when(me > 0)
     def _():
         greet(me - 1, core)
-        greet(me - 1, other)
 
     @pl.when(me < n - 1)
     def _():
         greet(me + 1, core)
-        greet(me + 1, other)
 
     for d in range(1, group):
         greet(inner_peer(d), core)
@@ -87,7 +85,7 @@
                 (dirs, dirs_v),
                 (taps, taps_v),
                 (wq, q_w),
-                (wo.at[:, my_out], o_w.at[core]),
+                (wo.at[:, my_out], o_w),
             ]
         )
     ]
@@ -102,7 +100,7 @@
     def _():
         x[reach + rows :, :] = jnp.zeros((reach, x.shape[1]), BF16)
 
-    sides = 2 * ((me > 0).astype(jnp.int32) + (me < n - 1).astype(jnp.int32))
+    sides = ((me > 0).astype(jnp.int32) + (me < n - 1).astype(jnp.int32))
     pl.semaphore_wait(barrier, outer - 1 + group + sides)
 
     def remote(src, dst, at, seq_id, core_id):
@@ -112,15 +110,19 @@
         )
 
     swap_tok = remote(tok, x.at[main, own_cols], 0, me, other)
-    lower = [
-        remote(tok.at[pl.ds(0, reach), :], x.at[pl.ds(reach + rows, reach), own_cols], 1 + k, me - 1, c)
-        for k, c in enumerate((core, other))
-    ]
-    upper = [
-        remote(tok.at[pl.ds(rows - reach, reach), :], x.at[pl.ds(0, reach), own_cols], 3 + k, me + 1, c)
-        for k, c in enumerate((core, other))
-    ]
-    swap_out = remote(wo.at[:, other_out], o_w.at[core], 5, me, other)
+    pieces = 2
+    part_rows = reach // pieces
+    lower, upper, lower_on, upper_on = [], [], [], []
+    for k in range(pieces):
+        low = x.at[pl.ds(reach + rows + k * part_rows, part_rows), own_cols]
+        high = x.at[pl.ds(k * part_rows, part_rows), own_cols]
+        lower.append(remote(tok.at[pl.ds(k * part_rows, part_rows), :], low, 4 + k, me - 1, core))
+        upper.append(
+            remote(tok.at[pl.ds(rows - reach + k * part_rows, part_rows), :], high, 6 + k, me + 1, core)
+        )
+        lower_on.append(remote(low, low, 8 + k, me, other))
+        upper_on.append(remote(high, high, 10 + k, me, other))
+    swap_out = remote(wo.at[:, other_out], o_w_in, 1, me, other)
 
     @pl.when(me > 0)
     def _():
@@ -133,7 +135,6 @@
             copy.start()
 
     swap_tok.start()
-    swap_out.start()
 
     dirs_hi[...] = jnp.zeros(dirs_hi.shape, BF16)
     dirs_lo[...] = jnp.zeros(dirs_lo.shape, BF16)
@@ -167,13 +168,25 @@
 
     @pl.when(me > 0)
     def _():
-        for copy in upper:
+        for copy, on in zip(upper, upper_on):
             copy.wait_recv()
+            on.start()
 
     @pl.when(me < n - 1)
     def _():
-        for copy in lower:
+        for copy, on in zip(lower, lower_on):
             copy.wait_recv()
+            on.start()
+
+    @pl.when(me > 0)
+    def _():
+        for on in upper_on:
+            on.wait_recv()
+
+    @pl.when(me < n - 1)
+    def _():
+        for on in lower_on:
+            on.wait_recv()
 
     keys[0:reach, :] = mm(x[0:reach, :], k_w[...]).astype(BF16)
     keys[reach + rows :, :] = mm(x[reach + rows :, :], k_w[...]).astype(BF16)
@@ -192,8 +205,6 @@
     c_hi, c_lo = split(c)
     kmix[...] = c_hi
     sq_hi, sq_lo = split(c * c)
-    out_keys = pltpu.make_async_copy(kmix, key_mixed, loc.at[7])
-    out_keys.start()
     logits = mm(c_hi, dirs_hi[...]) + mm(c_lo, dirs_hi[...]) + mm(c_hi, dirs_lo[...])
     logits = logits - (mm(sq_hi, norm_w[...]) + mm(sq_lo, norm_w[...]))
     kf = jnp.exp(logits).astype(BF16)
@@ -212,6 +223,7 @@
     ]
     for copy in scatter:
         copy.start()
+    swap_out.start()
     local[5].wait()
     queries[...] = mm(x[reach : reach + rows, :], q_w[...]).astype(BF16)
     mine = part[spot]
@@ -254,7 +266,7 @@
         s = slice(LANES + k * HEAD_DIM, LANES + (k + 1) * HEAD_DIM)
         f = slice(k * features, (k + 1) * features)
         gate[p, r, f] = full[h, 0:HEAD_DIM, :]
-        gate[p, s, f] = jnp.concatenate([full[h, HEAD_DIM:, :]] * (HEAD_DIM // PAD), axis=0)
+        gate[p, s, f] = jnp.broadcast_to(full[h, HEAD_DIM : HEAD_DIM + 1, :], (HEAD_DIM, features))
     steps = 2
     span = rows // steps
     swap_att = []
@@ -262,38 +274,43 @@
         r = slice(b * span, (b + 1) * span)
         for p in range(pairs):
             got = mm_nt(qf[r, 2 * p * features : 2 * (p + 1) * features], gate[p])
-            att[core, r, p * LANES : (p + 1) * LANES] = (got[:, :LANES] / got[:, LANES:]).astype(BF16)
-        piece = att.at[core, pl.ds(b * span, span), :]
-        copy = remote(piece, piece, 6 + b, me, other)
+            att[r, p * LANES : (p + 1) * LANES] = (got[:, :LANES] / got[:, LANES:]).astype(BF16)
+        piece = pl.ds(b * span, span)
+        copy = remote(att.at[piece, :], att_in.at[piece, :], 2 + b, me, other)
         copy.start()
         swap_att.append(copy)
     local[6].wait()
-    own = [mm(att[core, b * span : (b + 1) * span, :], o_w[core]) for b in range(steps)]
+    part_out[...] = mm(att[...], o_w[...])
     swap_out.wait_recv()
+    for copy in swap_att:
+        copy.wait_recv()
+    for copy in [swap_tok, swap_out] + scatter + spread + gather + swap_att:
+        copy.wait_send()
+
+    @pl.when(me > 0)
+    def _():
+        for copy in lower + upper_on:
+            copy.wait_send()
+
+    @pl.when(me < n - 1)
+    def _():
+        for copy in upper + lower_on:
+            copy.wait_send()
+
+
+def finish(part_in, att_in, o_w_in, kmix, mixed, key_mixed, out_v, sem):
+    rows = att_in.shape[0]
+    out_keys = pltpu.make_async_copy(kmix, key_mixed, sem.at[0])
+    out_keys.start()
     outs = []
+    steps = 2
+    span = rows // steps
     for b in range(steps):
         r = slice(b * span, (b + 1) * span)
-        swap_att[b].wait_recv()
-        out_v[r, :] = (own[b] + mm(att[other, r, :], o_w[other])).astype(BF16)
-        copy = pltpu.make_async_copy(
-            out_v.at[pl.ds(b * span, span), :], mixed.at[pl.ds(b * span, span), :], loc.at[8 + b]
-        )
-        copy.start()
-        outs.append(copy)
-
-    for copy in [swap_tok, swap_out] + scatter + spread + gather + swap_att:
-        copy.wait_send()
-
-    @pl.when(me > 0)
-    def _():
-        for copy in lower:
-            copy.wait_send()
-
-    @pl.when(me < n - 1)
-    def _():
-        for copy in upper:
-            copy.wait_send()
-
+        out_v[r, :] = (part_in[r, :] + mm(att_in[r, :], o_w_in[...])).astype(BF16)
+        piece = pl.ds(b * span, span)
+        outs.append(pltpu.make_async_copy(out_v.at[piece, :], mixed.at[piece, :], sem.at[1 + b]))
+        outs[b].start()
     out_keys.wait()
     for copy in outs:
         copy.wait()
@@ -313,20 +330,23 @@
     vmem = pltpu.VMEM
     dma = pltpu.SemaphoreType.DMA
     any_spec = pl.BlockSpec(memory_space=pl.ANY)
-    return pl.pallas_call(
+    vmem_spec = pl.BlockSpec(memory_space=pltpu.VMEM)
+    held = pl.pallas_call(
         functools.partial(fused, n, heads, reach),
         out_shape=(
-            jax.ShapeDtypeStruct((rows, out_cols), BF16),
-            jax.ShapeDtypeStruct((rows, width), BF16),
+            vmem((rows, out_cols), F32),
+            vmem((rows, width), BF16),
+            vmem((width, out_cols), BF16),
+            vmem((rows, width), BF16),
         ),
         in_specs=[any_spec] * 7,
-        out_specs=(any_spec, any_spec),
+        out_specs=(vmem_spec,) * 4,
         scratch_shapes=[
             vmem((rows + 2 * reach, d), BF16),
             vmem((d, width), BF16),
             vmem((d, width), BF16),
             vmem((d, width), BF16),
-            vmem((2, width, out_cols), BF16),
+            vmem((width, out_cols), BF16),
             vmem(feature_dirs.shape, F32),
             vmem(kernel_taps.shape, BF16),
             vmem((8, 2 * block), F32),
@@ -336,7 +356,6 @@
             vmem((width, heads * features), BF16),
             vmem((rows + 2 * reach, width), BF16),
             vmem((rows, width), F32),
-            vmem((rows, width), BF16),
             vmem((heads, chunk, rows), BF16),
             vmem((rows, width), BF16),
             vmem((rows, heads * features), BF16),
@@ -347,11 +366,10 @@
             vmem((max(outer - 1, 1), chunk, features), BF16),
             vmem((heads, chunk, features), BF16),
             vmem((width // LANES, 2 * LANES, 2 * features), BF16),
-            vmem((2, rows, width), BF16),
-            vmem((rows, out_cols), BF16),
-            dma((10,)),
-            dma((8,)),
-            dma((8,)),
+            vmem((rows, width), BF16),
+            dma((7,)),
+            dma((12,)),
+            dma((12,)),
             dma((heads - 1,)),
             dma((heads - 1,)),
             dma((max(outer - 1, 1),)),
@@ -362,6 +380,17 @@
         compiler_params=pltpu.CompilerParams(collective_id=0, has_side_effects=True),
         name="fused",
     )(tokens, w_query, w_key, w_value, w_out, feature_dirs, kernel_taps)
+    return pl.pallas_call(
+        finish,
+        out_shape=(
+            jax.ShapeDtypeStruct((rows, out_cols), BF16),
+            jax.ShapeDtypeStruct((rows, width), BF16),
+        ),
+        in_specs=[vmem_spec] * 4,
+        out_specs=(any_spec, any_spec),
+        scratch_shapes=[vmem((rows, out_cols), BF16), dma((3,))],
+        name="finish",
+    )(*[pltpu.with_memory_space_constraint(a, pltpu.VMEM) for a in held])
 
 
 def solution(mesh):

time: 28.6 us -> 25.2 us (0.88)
  the two profiles are of different devices: /device:TPU:1 before, /device:TPU:0 now
where the time goes in v2:
time: 25.2 us; the launch traced here: 25 us
  Pallas kernels  24.4 us (97%)
  between operations  0.64 us (3%)
    pallas_call x1, Pallas kernels, body(): pl.pallas_call(functools.partial(fused, n, heads, reach), out_shape=(vmem...  23.5 us
    pallas_call x1, Pallas kernels, body(): pl.pallas_call(finish, out_shape=(jax.ShapeDtypeStruct((rows, out_cols),...  0.89 us

profile of v2, /device:TPU:0, one launch (start us, length us, event | category | flops | bytes accessed | tf_op | source)
XLA Modules:
  0.0 25.0 jit_solution(2661333696547994975)
XLA Ops:
  0.6 23.5 %fused.1 = (f32[256,384]{1,0:T(8,128)S(1)}, bf16[256,256]{1,0:T(8,128)(2,1)S(1)}, bf16[256,384]{1,0:T(8,128)(2,1)S(1)}, bf16[256,256]{1,0:T(8,128)(2,1)S(1)}) custom-call(bf16[256,384]{1,0:T(8,128)(2,1)} %tok.1, bf16[768,256]{1,0:T(8,128)(2,1)} %wq.1, bf16[768,256]{1,0:T(8,128)(2,1)} %wk.1, bf16[768,256]{1,0:T(8,128)(2,1)} %wv.1, bf16[256,768]{1,0:T(8,128)(2,1)} %wo.1, ...), custom_call_target="tpu_custom_call" | custom-call | tf_op jit(solution)/shard_map/fused/pallas_call | solution.py:334
  24.1 0.9 %finish.1 = (bf16[256,384]{1,0:T(8,128)(2,1)}, bf16[256,256]{1,0:T(8,128)(2,1)}) custom-call(f32[256,384]{1,0:T(8,128)S(1)} %get-tuple-element.6.part_in, bf16[256,256]{1,0:T(8,128)(2,1)S(1)} %get-tuple-element.7.att_in, bf16[256,384]{1,0:T(8,128)(2,1)S(1)} %get-tuple-element.8.o_w_in, bf16[256,256]{1,0:T(8,128)(2,1)S(1)} %get-tuple-element.9.kmix), custom_call_target="tpu_custom_call" | custom-call | tf_op jit(solution)/shard_map/finish/pallas_call | solution.py:383

commit v3 on v2

--- a/solution.py
+++ b/solution.py
@@ -40,24 +40,42 @@
     pairs = width // LANES
     group, block = heads, 2 * reach
     outer = n // group
+    cuts = (pl.ds(0, HEAD_DIM // 2), pl.ds(HEAD_DIM // 2, HEAD_DIM // 2 + PAD))
     scale = HEAD_DIM ** (-0.25)
     me, core = lax.axis_index("seq"), lax.axis_index("head")
     other = 1 - core
     spot, plane = lax.rem(me, group), lax.div(me, group)
 
+    def inner_spot(d):
+        found, weight = 0, 1
+        while weight < group:
+            bit = lax.rem(lax.div(spot, weight), 2)
+            found = found + weight * (1 - bit if d & weight else bit)
+            weight *= 2
+        return found
+
     def inner_peer(d):
-        return plane * group + lax.rem(spot + d, group)
-
-    def outer_peer(e):
-        return lax.rem(plane + e, outer) * group + spot
+        return plane * group + inner_spot(d)
+
+    def other_plane(k):
+        return k + (plane <= k).astype(jnp.int32)
+
+    low_side = (2 * plane < outer).astype(jnp.int32)
+
+    def far_plane(k):
+        top = outer - 1 - k
+        return low_side * (top - (plane >= top).astype(jnp.int32)) + (1 - low_side) * other_plane(k)
+
+    def outer_peer(k):
+        return far_plane(k) * group + spot
 
     barrier = pltpu.get_barrier_semaphore()
 
     def greet(seq_id, core_id):
         pl.semaphore_signal(barrier, inc=1, device_id=(seq_id, core_id), device_id_type=MESH)
 
-    for e in range(1, outer):
-        greet(outer_peer(e), core)
+    for k in range(outer - 1):
+        greet(outer_peer(k), core)
 
     @pl.when(me > 0)
     def _():
@@ -213,50 +231,61 @@
         part[h] = got
         part_b[h] = got.astype(BF16)
 
+    order = range(group - 1, 0, -1)
     scatter = [
-        pltpu.make_async_remote_copy(
-            src_ref=part_b.at[lax.rem(spot + d, group)], dst_ref=inner_in.at[d - 1],
-            send_sem=inner_send.at[d - 1], recv_sem=inner_recv.at[d - 1],
-            device_id=(inner_peer(d), core), device_id_type=MESH,
-        )
-        for d in range(1, group)
+        [
+            pltpu.make_async_remote_copy(
+                src_ref=part_b.at[inner_spot(d), at, :], dst_ref=inner_in.at[d - 1, at, :],
+                send_sem=inner_send.at[t, d - 1], recv_sem=inner_recv.at[t, d - 1],
+                device_id=(inner_peer(d), core), device_id_type=MESH,
+            )
+            for d in order
+        ]
+        for t, at in enumerate(cuts)
     ]
-    for copy in scatter:
+    for copy in scatter[0] + scatter[1]:
         copy.start()
     swap_out.start()
     local[5].wait()
     queries[...] = mm(x[reach : reach + rows, :], q_w[...]).astype(BF16)
-    mine = part[spot]
-    for d in range(1, group):
-        scatter[d - 1].wait_recv()
-        mine = mine + inner_in[d - 1].astype(F32)
-    outer_b[...] = mine.astype(BF16)
-    spread = [
-        pltpu.make_async_remote_copy(
-            src_ref=outer_b, dst_ref=outer_in.at[e - 1],
-            send_sem=outer_send.at[e - 1], recv_sem=outer_recv.at[e - 1],
-            device_id=(outer_peer(e), core), device_id_type=MESH,
-        )
-        for e in range(1, outer)
-    ]
-    for copy in spread:
-        copy.start()
+    spread, sums = [], []
+    for t, at in enumerate(cuts):
+        mine = part[spot, at, :]
+        for copy, d in zip(scatter[t], order):
+            copy.wait_recv()
+            mine = mine + inner_in[d - 1, at, :].astype(F32)
+        outer_b[at, :] = mine.astype(BF16)
+        sums.append(mine)
+        for k in range(outer - 1):
+            copy = pltpu.make_async_remote_copy(
+                src_ref=outer_b.at[at, :], dst_ref=outer_in.at[plane, at, :],
+                send_sem=outer_send.at[t, k], recv_sem=outer_recv.at[t, plane],
+                device_id=(outer_peer(k), core), device_id_type=MESH,
+            )
+            copy.start()
+            spread.append(copy)
     q = queries[...]
     qf[...] = jnp.exp(mm(q, dirs_hi[...]) + mm(q, dirs_lo[...])).astype(BF16)
-    for e in range(1, outer):
-        spread[e - 1].wait_recv()
-        mine = mine + outer_in[e - 1].astype(F32)
-    full[spot] = mine.astype(BF16)
-    gather = [
-        pltpu.make_async_remote_copy(
-            src_ref=full.at[spot], dst_ref=full.at[spot],
-            send_sem=full_send.at[d - 1], recv_sem=full_recv.at[d - 1],
-            device_id=(inner_peer(d), core), device_id_type=MESH,
-        )
-        for d in range(1, group)
-    ]
-    for copy in gather:
-        copy.start()
+    gather = []
+    for t, at in enumerate(cuts):
+        mine = sums[t]
+        for k in range(outer - 1):
+            source = other_plane(k)
+            pltpu.make_async_remote_copy(
+                src_ref=outer_b.at[at, :], dst_ref=outer_in.at[source, at, :],
+                send_sem=outer_send.at[t, k], recv_sem=outer_recv.at[t, source],
+                device_id=(outer_peer(k), core), device_id_type=MESH,
+            ).wait_recv()
+            mine = mine + outer_in[source, at, :].astype(F32)
+        full[spot, at, :] = mine.astype(BF16)
+        for d in order:
+            copy = pltpu.make_async_remote_copy(
+                src_ref=full.at[spot, at, :], dst_ref=full.at[spot, at, :],
+                send_sem=full_send.at[t, d - 1], recv_sem=full_recv.at[t, d - 1],
+                device_id=(inner_peer(d), core), device_id_type=MESH,
+            )
+            copy.start()
+            gather.append(copy)
     for copy in gather:
         copy.wait_recv()
 
@@ -284,7 +313,7 @@
     swap_out.wait_recv()
     for copy in swap_att:
         copy.wait_recv()
-    for copy in [swap_tok, swap_out] + scatter + spread + gather + swap_att:
+    for copy in [swap_tok, swap_out] + scatter[0] + scatter[1] + spread + gather + swap_att:
         copy.wait_send()
 
     @pl.when(me > 0)
@@ -363,19 +392,19 @@
             vmem((heads, chunk, features), BF16),
             vmem((heads - 1, chunk, features), BF16),
             vmem((chunk, features), BF16),
-            vmem((max(outer - 1, 1), chunk, features), BF16),
+            vmem((outer, chunk, features), BF16),
             vmem((heads, chunk, features), BF16),
             vmem((width // LANES, 2 * LANES, 2 * features), BF16),
             vmem((rows, width), BF16),
             dma((7,)),
             dma((12,)),
             dma((12,)),
-            dma((heads - 1,)),
-            dma((heads - 1,)),
-            dma((max(outer - 1, 1),)),
-            dma((max(outer - 1, 1),)),
-            dma((heads - 1,)),
-            dma((heads - 1,)),
+            dma((2, heads - 1)),
+            dma((2, heads - 1)),
+            dma((2, max(outer - 1, 1))),
+            dma((2, outer)),
+            dma((2, heads - 1)),
+            dma((2, heads - 1)),
         ],
         compiler_params=pltpu.CompilerParams(collective_id=0, has_side_effects=True),
         name="fused",

time: 25.2 us -> 25.1 us (level)
  no operation moved by 1% of the time
where the time goes in v3:
time: 25.1 us; the launch traced here: 25 us
  Pallas kernels  24.3 us (97%)
  between operations  0.64 us (3%)
    pallas_call x1, Pallas kernels, body(): pl.pallas_call(functools.partial(fused, n, heads, reach), out_shape=(vmem...  23.4 us
    pallas_call x1, Pallas kernels, body(): pl.pallas_call(finish, out_shape=(jax.ShapeDtypeStruct((rows, out_cols),...  0.89 us

profile of v3, /device:TPU:0, one launch (start us, length us, event | category | flops | bytes accessed | tf_op | source)
XLA Modules:
  0.0 25.0 jit_solution(16342626451650927202)
XLA Ops:
  0.6 23.4 %fused.1 = (f32[256,384]{1,0:T(8,128)S(1)}, bf16[256,256]{1,0:T(8,128)(2,1)S(1)}, bf16[256,384]{1,0:T(8,128)(2,1)S(1)}, bf16[256,256]{1,0:T(8,128)(2,1)S(1)}) custom-call(bf16[256,384]{1,0:T(8,128)(2,1)} %tok.1, bf16[768,256]{1,0:T(8,128)(2,1)} %wq.1, bf16[768,256]{1,0:T(8,128)(2,1)} %wk.1, bf16[768,256]{1,0:T(8,128)(2,1)} %wv.1, bf16[256,768]{1,0:T(8,128)(2,1)} %wo.1, ...), custom_call_target="tpu_custom_call" | custom-call | tf_op jit(solution)/shard_map/fused/pallas_call | solution.py:363
  24.1 0.9 %finish.1 = (bf16[256,384]{1,0:T(8,128)(2,1)}, bf16[256,256]{1,0:T(8,128)(2,1)}) custom-call(f32[256,384]{1,0:T(8,128)S(1)} %get-tuple-element.6.part_in, bf16[256,256]{1,0:T(8,128)(2,1)S(1)} %get-tuple-element.7.att_in, bf16[256,384]{1,0:T(8,128)(2,1)S(1)} %get-tuple-element.8.o_w_in, bf16[256,256]{1,0:T(8,128)(2,1)S(1)} %get-tuple-element.9.kmix), custom_call_target="tpu_custom_call" | custom-call | tf_op jit(solution)/shard_map/finish/pallas_call | solution.py:412

commit v4 on v3

--- a/solution.py
+++ b/solution.py
@@ -30,7 +30,7 @@
 def fused(
     n, heads, reach, tok, wq, wk, wv, wo, dirs, taps, part_out, att_in, o_w_in, kmix,
     x, q_w, k_w, v_w, o_w, dirs_v, taps_v, taps_pad, band, dirs_hi, dirs_lo, norm_w,
-    keys, conv, vt, queries, qf, part, part_b, inner_in, outer_b, outer_in, full, gate, att,
+    keys, vt, queries, qf, part, part_b, inner_in, outer_b, outer_in, full, gate, att,
     loc, send, recv, inner_send, inner_recv, outer_send, outer_recv, full_send, full_recv,
 ):
     rows, half = tok.shape
@@ -40,7 +40,7 @@
     pairs = width // LANES
     group, block = heads, 2 * reach
     outer = n // group
-    cuts = (pl.ds(0, HEAD_DIM // 2), pl.ds(HEAD_DIM // 2, HEAD_DIM // 2 + PAD))
+    cuts = (pl.ds(0, HEAD_DIM + PAD),)
     scale = HEAD_DIM ** (-0.25)
     me, core = lax.axis_index("seq"), lax.axis_index("head")
     other = 1 - core
@@ -180,9 +180,35 @@
     swap_tok.wait_recv()
     keys[reach : reach + rows, :] = mm(x[reach : reach + rows, :], k_w[...]).astype(BF16)
     local[2].wait()
-    values_t = mm(x[reach : reach + rows, :], v_w[...]).T.astype(BF16)
+    values = mm(x[reach : reach + rows, :], v_w[...])
+    values_t = jnp.concatenate([values[reach : rows - reach], values[:reach], values[rows - reach :]], axis=0).T
+    values_t = values_t.astype(BF16)
     for h in range(heads):
         vt[h, 0:HEAD_DIM, :] = values_t[h * HEAD_DIM : (h + 1) * HEAD_DIM, :]
+
+    lane = lax.broadcasted_iota(jnp.int32, (block, LANES), 1)
+
+    def key_feats(c):
+        c_hi, c_lo = split(c)
+        sq_hi, sq_lo = split(c * c)
+        logits = mm(c_hi, dirs_hi[...]) + mm(c_lo, dirs_hi[...]) + mm(c_hi, dirs_lo[...])
+        logits = logits - (mm(sq_hi, norm_w[...]) + mm(sq_lo, norm_w[...]))
+        return c_hi, jnp.exp(logits).astype(BF16)
+
+    inside = rows - block
+    for b in range(inside // block):
+        sides_of = []
+        for p in range(pairs):
+            got = mm(
+                band[2 * p * block : 2 * (p + 1) * block, :],
+                keys[reach + b * block : reach + (b + 2) * block, p * LANES : (p + 1) * LANES],
+            )
+            sides_of.append(jnp.where(lane < HEAD_DIM, got[:block], got[block:]))
+        mix, kf = key_feats(jnp.concatenate(sides_of, axis=1))
+        kmix[reach + b * block : reach + (b + 1) * block, :] = mix
+        for h in range(heads):
+            got = mm(vt[h, :, b * block : (b + 1) * block], kf[:, h * features : (h + 1) * features])
+            part[h] = got if b == 0 else part[h] + got
 
     @pl.when(me > 0)
     def _():
@@ -206,28 +232,28 @@
         for on in lower_on:
             on.wait_recv()
 
-    keys[0:reach, :] = mm(x[0:reach, :], k_w[...]).astype(BF16)
-    keys[reach + rows :, :] = mm(x[reach + rows :, :], k_w[...]).astype(BF16)
-
-    lane = lax.broadcasted_iota(jnp.int32, (block, LANES), 1)
-    for b in range(rows // block):
-        for p in range(pairs):
-            got = mm(
-                band[2 * p * block : 2 * (p + 1) * block, :],
-                keys[b * block : (b + 2) * block, p * LANES : (p + 1) * LANES],
-            )
-            conv[b * block : (b + 1) * block, p * LANES : (p + 1) * LANES] = jnp.where(
-                lane < HEAD_DIM, got[:block], got[block:]
-            )
-    c = conv[...]
-    c_hi, c_lo = split(c)
-    kmix[...] = c_hi
-    sq_hi, sq_lo = split(c * c)
-    logits = mm(c_hi, dirs_hi[...]) + mm(c_lo, dirs_hi[...]) + mm(c_hi, dirs_lo[...])
-    logits = logits - (mm(sq_hi, norm_w[...]) + mm(sq_lo, norm_w[...]))
-    kf = jnp.exp(logits).astype(BF16)
-    for h in range(heads):
-        got = mm(vt[h], kf[:, h * features : (h + 1) * features])
+    ends = mm(jnp.concatenate([x[0:reach, :], x[reach + rows :, :]], axis=0), k_w[...]).astype(BF16)
+    span3 = 3 * reach
+    low_keys = jnp.concatenate([ends[:reach], keys[reach:span3, :]], axis=0)
+    high_keys = jnp.concatenate([keys[rows - reach : rows + reach, :], ends[reach:]], axis=0)
+    edge = lane[:reach] < HEAD_DIM
+    lows, highs = [], []
+    for p in range(pairs):
+        r, cols = 2 * p * block, slice(p * LANES, (p + 1) * LANES)
+        taps_two = jnp.concatenate(
+            [band[r : r + reach, :span3], band[r + block : r + block + reach, :span3]], axis=0
+        )
+        got = mm(taps_two, jnp.concatenate([low_keys[:, cols], high_keys[:, cols]], axis=1))
+        lows.append(jnp.where(edge, got[:reach, :LANES], got[reach:, :LANES]))
+        highs.append(jnp.where(edge, got[:reach, LANES:], got[reach:, LANES:]))
+    mix, kf = key_feats(
+        jnp.concatenate([jnp.concatenate(lows, axis=1), jnp.concatenate(highs, axis=1)], axis=0)
+    )
+    kmix[0:reach, :] = mix[:reach]
+    kmix[rows - reach :, :] = mix[reach:]
+    for h in range(heads):
+        got = mm(vt[h, :, inside:], kf[:, h * features : (h + 1) * features])
+        got = part[h] + got if inside else got
         part[h] = got
         part_b[h] = got.astype(BF16)
 
@@ -243,7 +269,7 @@
         ]
         for t, at in enumerate(cuts)
     ]
-    for copy in scatter[0] + scatter[1]:
+    for copy in sum(scatter, []):
         copy.start()
     swap_out.start()
     local[5].wait()
@@ -313,7 +339,7 @@
     swap_out.wait_recv()
     for copy in swap_att:
         copy.wait_recv()
-    for copy in [swap_tok, swap_out] + scatter[0] + scatter[1] + spread + gather + swap_att:
+    for copy in [swap_tok, swap_out] + sum(scatter, []) + spread + gather + swap_att:
         copy.wait_send()
 
     @pl.when(me > 0)
@@ -384,7 +410,6 @@
             vmem((width, heads * features), BF16),
             vmem((width, heads * features), BF16),
             vmem((rows + 2 * reach, width), BF16),
-            vmem((rows, width), F32),
             vmem((heads, chunk, rows), BF16),
             vmem((rows, width), BF16),
             vmem((rows, heads * features), BF16),
@@ -399,12 +424,12 @@
             dma((7,)),
             dma((12,)),
             dma((12,)),
-            dma((2, heads - 1)),
-            dma((2, heads - 1)),
-            dma((2, max(outer - 1, 1))),
-            dma((2, outer)),
-            dma((2, heads - 1)),
-            dma((2, heads - 1)),
+            dma((1, heads - 1)),
+            dma((1, heads - 1)),
+            dma((1, max(outer - 1, 1))),
+            dma((1, outer)),
+            dma((1, heads - 1)),
+            dma((1, heads - 1)),
         ],
         compiler_params=pltpu.CompilerParams(collective_id=0, has_side_effects=True),
         name="fused",

time: 25.1 us -> 24.7 us (0.984)
  Pallas kernels: 24.3 us -> 24 us
    pallas_call x1, Pallas kernels: 23.4 us -> 23.1 us  [body(): pl.pallas_call(functools.partial(fused, n, heads, reach), out_shape=(vmem...]
where the time goes in v4:
time: 24.7 us; the launch traced here: 24.6 us
  Pallas kernels  24 us (97%)
  between operations  0.64 us (3%)
    pallas_call x1, Pallas kernels, body(): pl.pallas_call(functools.partial(fused, n, heads, reach), out_shape=(vmem...  23.1 us
    pallas_call x1, Pallas kernels, body(): pl.pallas_call(finish, out_shape=(jax.ShapeDtypeStruct((rows, out_cols),...  0.9 us

profile of v4, /device:TPU:0, one launch (start us, length us, event | category | flops | bytes accessed | tf_op | source)
XLA Modules:
  0.0 24.6 jit_solution(1041171074660987616)
XLA Ops:
  0.6 23.1 %fused.1 = (f32[256,384]{1,0:T(8,128)S(1)}, bf16[256,256]{1,0:T(8,128)(2,1)S(1)}, bf16[256,384]{1,0:T(8,128)(2,1)S(1)}, bf16[256,256]{1,0:T(8,128)(2,1)S(1)}) custom-call(bf16[256,384]{1,0:T(8,128)(2,1)} %tok.1, bf16[768,256]{1,0:T(8,128)(2,1)} %wq.1, bf16[768,256]{1,0:T(8,128)(2,1)} %wk.1, bf16[768,256]{1,0:T(8,128)(2,1)} %wv.1, bf16[256,768]{1,0:T(8,128)(2,1)} %wo.1, ...), custom_call_target="tpu_custom_call" | custom-call | tf_op jit(solution)/shard_map/fused/pallas_call | solution.py:389
  23.7 0.9 %finish.1 = (bf16[256,384]{1,0:T(8,128)(2,1)}, bf16[256,256]{1,0:T(8,128)(2,1)}) custom-call(f32[256,384]{1,0:T(8,128)S(1)} %get-tuple-element.6.part_in, bf16[256,256]{1,0:T(8,128)(2,1)S(1)} %get-tuple-element.7.att_in, bf16[256,384]{1,0:T(8,128)(2,1)S(1)} %get-tuple-element.8.o_w_in, bf16[256,256]{1,0:T(8,128)(2,1)S(1)} %get-tuple-element.9.kmix), custom_call_target="tpu_custom_call" | custom-call | tf_op jit(solution)/shard_map/finish/pallas_call | solution.py:437

commit v5 on v4

--- a/solution.py
+++ b/solution.py
@@ -28,14 +28,14 @@
 
 
 def fused(
-    n, heads, reach, tok, wq, wk, wv, wo, dirs, taps, part_out, att_in, o_w_in, kmix,
-    x, q_w, k_w, v_w, o_w, dirs_v, taps_v, taps_pad, band, dirs_hi, dirs_lo, norm_w,
-    keys, vt, queries, qf, part, part_b, inner_in, outer_b, outer_in, full, gate, att,
+    n, heads, reach, tok, wq, wk, wv, wo, dirs, taps, qf, qf_in, gate, gate_in, o_w, o_w_in, kmix,
+    x, q_w, k_w, v_w, dirs_v, taps_v, taps_pad, band, dirs_hi, dirs_lo, norm_w,
+    keys, vt, queries, part, part_b, inner_in, outer_b, outer_in, full, full_in,
     loc, send, recv, inner_send, inner_recv, outer_send, outer_recv, full_send, full_recv,
 ):
     rows, half = tok.shape
     features = dirs.shape[1]
-    out_cols = part_out.shape[1]
+    out_cols = o_w.shape[1]
     width = heads * HEAD_DIM
     pairs = width // LANES
     group, block = heads, 2 * reach
@@ -87,6 +87,7 @@
 
     for d in range(1, group):
         greet(inner_peer(d), core)
+        greet(inner_peer(d), other)
     greet(me, other)
 
     own_cols = pl.ds(pl.multiple_of(core * half, LANES), half)
@@ -119,7 +120,7 @@
         x[reach + rows :, :] = jnp.zeros((reach, x.shape[1]), BF16)
 
     sides = ((me > 0).astype(jnp.int32) + (me < n - 1).astype(jnp.int32))
-    pl.semaphore_wait(barrier, outer - 1 + group + sides)
+    pl.semaphore_wait(barrier, outer - 1 + 2 * group - 1 + sides)
 
     def remote(src, dst, at, seq_id, core_id):
         return pltpu.make_async_remote_copy(
@@ -158,6 +159,7 @@
     dirs_lo[...] = jnp.zeros(dirs_lo.shape, BF16)
     norm_w[...] = jnp.zeros(norm_w.shape, BF16)
     gate[...] = jnp.zeros(gate.shape, BF16)
+    gate_in[...] = jnp.zeros(gate_in.shape, BF16)
     taps_pad[...] = jnp.zeros(taps_pad.shape, F32)
     for h in range(heads):
         r, c = slice(h * HEAD_DIM, (h + 1) * HEAD_DIM), slice(h * features, (h + 1) * features)
@@ -292,6 +294,8 @@
             spread.append(copy)
     q = queries[...]
     qf[...] = jnp.exp(mm(q, dirs_hi[...]) + mm(q, dirs_lo[...])).astype(BF16)
+    swap_qf = remote(qf, qf_in, 2, me, other)
+    swap_qf.start()
     gather = []
     for t, at in enumerate(cuts):
         mine = sums[t]
@@ -304,42 +308,30 @@
             ).wait_recv()
             mine = mine + outer_in[source, at, :].astype(F32)
         full[spot, at, :] = mine.astype(BF16)
-        for d in order:
+        targets = [(inner_peer(d), side) for d in order for side in (other, core)] + [(me, other)]
+        for k, target in enumerate(targets):
+            home = full if k % 2 and k < 2 * group - 2 else full_in
             copy = pltpu.make_async_remote_copy(
-                src_ref=full.at[spot, at, :], dst_ref=full.at[spot, at, :],
-                send_sem=full_send.at[t, d - 1], recv_sem=full_recv.at[t, d - 1],
-                device_id=(inner_peer(d), core), device_id_type=MESH,
+                src_ref=full.at[spot, at, :], dst_ref=home.at[spot, at, :],
+                send_sem=full_send.at[t, k], recv_sem=full_recv.at[t, k],
+                device_id=target, device_id_type=MESH,
             )
             copy.start()
             gather.append(copy)
+    local[6].wait()
+    swap_out.wait_recv()
+    swap_qf.wait_recv()
     for copy in gather:
         copy.wait_recv()
-
-    for h in range(heads):
-        p, k = divmod(h, 2)
-        r = slice(k * HEAD_DIM, (k + 1) * HEAD_DIM)
-        s = slice(LANES + k * HEAD_DIM, LANES + (k + 1) * HEAD_DIM)
-        f = slice(k * features, (k + 1) * features)
-        gate[p, r, f] = full[h, 0:HEAD_DIM, :]
-        gate[p, s, f] = jnp.broadcast_to(full[h, HEAD_DIM : HEAD_DIM + 1, :], (HEAD_DIM, features))
-    steps = 2
-    span = rows // steps
-    swap_att = []
-    for b in range(steps):
-        r = slice(b * span, (b + 1) * span)
-        for p in range(pairs):
-            got = mm_nt(qf[r, 2 * p * features : 2 * (p + 1) * features], gate[p])
-            att[r, p * LANES : (p + 1) * LANES] = (got[:, :LANES] / got[:, LANES:]).astype(BF16)
-        piece = pl.ds(b * span, span)
-        copy = remote(att.at[piece, :], att_in.at[piece, :], 2 + b, me, other)
-        copy.start()
-        swap_att.append(copy)
-    local[6].wait()
-    part_out[...] = mm(att[...], o_w[...])
-    swap_out.wait_recv()
-    for copy in swap_att:
-        copy.wait_recv()
-    for copy in [swap_tok, swap_out] + sum(scatter, []) + spread + gather + swap_att:
+    for home, door in ((full, gate), (full_in, gate_in)):
+        for h in range(heads):
+            p, k = divmod(h, 2)
+            r = slice(k * HEAD_DIM, (k + 1) * HEAD_DIM)
+            s = slice(LANES + k * HEAD_DIM, LANES + (k + 1) * HEAD_DIM)
+            f = slice(k * features, (k + 1) * features)
+            door[p, r, f] = home[h, 0:HEAD_DIM, :]
+            door[p, s, f] = jnp.broadcast_to(home[h, HEAD_DIM : HEAD_DIM + 1, :], (HEAD_DIM, features))
+    for copy in [swap_tok, swap_out, swap_qf] + sum(scatter, []) + spread + gather:
         copy.wait_send()
 
     @pl.when(me > 0)
@@ -353,16 +345,25 @@
             copy.wait_send()
 
 
-def finish(part_in, att_in, o_w_in, kmix, mixed, key_mixed, out_v, sem):
-    rows = att_in.shape[0]
+def finish(qf, qf_in, gate, gate_in, o_w, o_w_in, kmix, mixed, key_mixed, out_v, sem):
+    rows = qf.shape[0]
     out_keys = pltpu.make_async_copy(kmix, key_mixed, sem.at[0])
     out_keys.start()
     outs = []
     steps = 2
     span = rows // steps
+    pairs, _, deep = gate.shape
     for b in range(steps):
         r = slice(b * span, (b + 1) * span)
-        out_v[r, :] = (part_in[r, :] + mm(att_in[r, :], o_w_in[...])).astype(BF16)
+        total = None
+        for feats, door, w in ((qf, gate, o_w), (qf_in, gate_in, o_w_in)):
+            att = []
+            for p in range(pairs):
+                got = mm_nt(feats[r, p * deep : (p + 1) * deep], door[p])
+                att.append((got[:, :LANES] / got[:, LANES:]).astype(BF16))
+            got = mm(jnp.concatenate(att, axis=1), w[...])
+            total = got if total is None else total + got
+        out_v[r, :] = total.astype(BF16)
         piece = pl.ds(b * span, span)
         outs.append(pltpu.make_async_copy(out_v.at[piece, :], mixed.at[piece, :], sem.at[1 + b]))
         outs[b].start()
@@ -389,19 +390,21 @@
     held = pl.pallas_call(
         functools.partial(fused, n, heads, reach),
         out_shape=(
-            vmem((rows, out_cols), F32),
-            vmem((rows, width), BF16),
+            vmem((rows, heads * features), BF16),
+            vmem((rows, heads * features), BF16),
+            vmem((width // LANES, 2 * LANES, 2 * features), BF16),
+            vmem((width // LANES, 2 * LANES, 2 * features), BF16),
+            vmem((width, out_cols), BF16),
             vmem((width, out_cols), BF16),
             vmem((rows, width), BF16),
         ),
         in_specs=[any_spec] * 7,
-        out_specs=(vmem_spec,) * 4,
+        out_specs=(vmem_spec,) * 7,
         scratch_shapes=[
             vmem((rows + 2 * reach, d), BF16),
             vmem((d, width), BF16),
             vmem((d, width), BF16),
             vmem((d, width), BF16),
-            vmem((width, out_cols), BF16),
             vmem(feature_dirs.shape, F32),
             vmem(kernel_taps.shape, BF16),
             vmem((8, 2 * block), F32),
@@ -412,15 +415,13 @@
             vmem((rows + 2 * reach, width), BF16),
             vmem((heads, chunk, rows), BF16),
             vmem((rows, width), BF16),
-            vmem((rows, heads * features), BF16),
             vmem((heads, chunk, features), F32),
             vmem((heads, chunk, features), BF16),
             vmem((heads - 1, chunk, features), BF16),
             vmem((chunk, features), BF16),
             vmem((outer, chunk, features), BF16),
             vmem((heads, chunk, features), BF16),
-            vmem((width // LANES, 2 * LANES, 2 * features), BF16),
-            vmem((rows, width), BF16),
+            vmem((heads, chunk, features), BF16),
             dma((7,)),
             dma((12,)),
             dma((12,)),
@@ -428,8 +429,8 @@
             dma((1, heads - 1)),
             dma((1, max(outer - 1, 1))),
             dma((1, outer)),
-            dma((1, heads - 1)),
-            dma((1, heads - 1)),
+            dma((1, 2 * heads - 1)),
+            dma((1, 2 * heads - 1)),
         ],
         compiler_params=pltpu.CompilerParams(collective_id=0, has_side_effects=True),
         name="fused",
@@ -440,7 +441,7 @@
             jax.ShapeDtypeStruct((rows, out_cols), BF16),
             jax.ShapeDtypeStruct((rows, width), BF16),
         ),
-        in_specs=[vmem_spec] * 4,
+        in_specs=[vmem_spec] * 7,
         out_specs=(any_spec, any_spec),
         scratch_shapes=[vmem((rows, out_cols), BF16), dma((3,))],
         name="finish",

time: 24.7 us -> 24.3 us (0.984)
  Pallas kernels: 24 us -> 23.5 us
    pallas_call x1, Pallas kernels: 23.1 us -> 22.1 us  [body(): pl.pallas_call(functools.partial(fused, n, heads, reach), out_shape=(vmem...]
    pallas_call x1, Pallas kernels: 0.9 us -> 1.5 us  [body(): pl.pallas_call(finish, out_shape=(jax.ShapeDtypeStruct((rows, out_cols),...]
where the time goes in v5:
time: 24.3 us; the launch traced here: 24.2 us
  Pallas kernels  23.5 us (97%)
  between operations  0.64 us (3%)
    pallas_call x1, Pallas kernels, body(): pl.pallas_call(functools.partial(fused, n, heads, reach), out_shape=(vmem...  22.1 us
    pallas_call x1, Pallas kernels, body(): pl.pallas_call(finish, out_shape=(jax.ShapeDtypeStruct((rows, out_cols),...  1.5 us

profile of v5, /device:TPU:0, one launch (start us, length us, event | category | flops | bytes accessed | tf_op | source)
XLA Modules:
  0.0 24.2 jit_solution(3180992838743808840)
XLA Ops:
  0.6 22.1 %fused.1 = (bf16[256,512]{1,0:T(8,128)(2,1)S(1)}, bf16[256,512]{1,0:T(8,128)(2,1)S(1)}, bf16[2,256,256]{2,1,0:T(8,128)(2,1)S(1)}, bf16[2,256,256]{2,1,0:T(8,128)...) custom-call(bf16[256,384]{1,0:T(8,128)(2,1)} %tok.1, ...), custom_call_target="tpu_custom_call" | custom-call | tf_op jit(solution)/shard_map/fused/pallas_call | solution.py:390
  22.7 1.5 %finish.1 = (bf16[256,384]{1,0:T(8,128)(2,1)}, bf16[256,256]{1,0:T(8,128)(2,1)}) custom-call(bf16[256,512]{1,0:T(8,128)(2,1)S(1)} %get-tuple-element.9.qf, bf16[256,512]{1,0:T(8,128)(2,1)S(1)} %get-tuple-element.10.qf_in, bf16[2,256,256]{2,1,0:T(8,128)(2,1)S(1)} %get-tuple-element.11.gate, bf16[2,256,256]{2,1,0:T(8,128)(2,1)S(1)} %get-tuple-element.12.gate_in, ...), custom_call_target="tpu_custom_call" | custom-call | tf_op jit(solution)/shard_map/finish/pallas_call | solution.py:438

commit v6 on v5

--- a/solution.py
+++ b/solution.py
@@ -143,12 +143,19 @@
         upper_on.append(remote(high, high, 10 + k, me, other))
     swap_out = remote(wo.at[:, other_out], o_w_in, 1, me, other)
 
+    odd = lax.rem(me, 2)
+
+    @pl.when((me < n - 1) & (odd == 1))
+    def _():
+        for copy in upper:
+            copy.start()
+
     @pl.when(me > 0)
     def _():
         for copy in lower:
             copy.start()
 
-    @pl.when(me < n - 1)
+    @pl.when((me < n - 1) & (odd == 0))
     def _():
         for copy in upper:
             copy.start()

time: 24.3 us -> 24.3 us (level)
  no operation moved by 1% of the time
where the time goes in v6:
time: 24.3 us; the launch traced here: 24.2 us
  Pallas kernels  23.5 us (97%)
  between operations  0.64 us (3%)
    pallas_call x1, Pallas kernels, body(): pl.pallas_call(functools.partial(fused, n, heads, reach), out_shape=(vmem...  22.1 us
    pallas_call x1, Pallas kernels, body(): pl.pallas_call(finish, out_shape=(jax.ShapeDtypeStruct((rows, out_cols),...  1.5 us

profile of v6, /device:TPU:0, one launch (start us, length us, event | category | flops | bytes accessed | tf_op | source)
XLA Modules:
  0.0 24.2 jit_solution(12322723672987612193)
XLA Ops:
  0.6 22.1 %fused.1 = (bf16[256,512]{1,0:T(8,128)(2,1)S(1)}, bf16[256,512]{1,0:T(8,128)(2,1)S(1)}, bf16[2,256,256]{2,1,0:T(8,128)(2,1)S(1)}, bf16[2,256,256]{2,1,0:T(8,128)...) custom-call(bf16[256,384]{1,0:T(8,128)(2,1)} %tok.1, ...), custom_call_target="tpu_custom_call" | custom-call | tf_op jit(solution)/shard_map/fused/pallas_call | solution.py:397
  22.7 1.5 %finish.1 = (bf16[256,384]{1,0:T(8,128)(2,1)}, bf16[256,256]{1,0:T(8,128)(2,1)}) custom-call(bf16[256,512]{1,0:T(8,128)(2,1)S(1)} %get-tuple-element.9.qf, bf16[256,512]{1,0:T(8,128)(2,1)S(1)} %get-tuple-element.10.qf_in, bf16[2,256,256]{2,1,0:T(8,128)(2,1)S(1)} %get-tuple-element.11.gate, bf16[2,256,256]{2,1,0:T(8,128)(2,1)S(1)} %get-tuple-element.12.gate_in, ...), custom_call_target="tpu_custom_call" | custom-call | tf_op jit(solution)/shard_map/finish/pallas_call | solution.py:445
